TPU v7x, 32 devices: a whole 2x2x4 slice. The times are simulated.
32 devices in a mesh: query: 2 (over y), dom: 16 (over z, x, core).
Axes of the slice: x: 2, y: 2, z: 4, core: 2. Of those that a mesh axis runs over, the one named last changes fastest.
Arguments:
- h_in: bfloat16 [4096, 256], P('dom', 'query'), may hold values from -6 to 6
- cotangent: bfloat16 [4096, 256], P('dom', 'query'), may hold values from -6 to 6
- w_one: bfloat16 [64, 64], replicated, may hold values from -0.75 to 0.75
- w_two: bfloat16 [64, 64], replicated, may hold values from -0.75 to 0.75
- rel_one: bfloat16 [535, 64], replicated, may hold values from -3 to 3
- rel_two: bfloat16 [535, 64], replicated, may hold values from -3 to 3
- query_emb: bfloat16 [535, 64], replicated, may hold values from -6 to 6
- q_head: int32 [4], P('query'), may hold values from 0 to 4095
- q_rel: int32 [4], P('query'), may hold values from 0 to 534
- bnd_rows: int32 [1024], P('dom'), may hold values from 0 to 255
- ghost_slots: int32 [256, 16], P('dom'), may hold values from 0 to 63
- edges_in: int32 [3, 16384], P(None, 'dom'), may hold values from 0 to 535, as said below
- edges_bd: int32 [3, 16384], P(None, 'dom'), may hold values from 0 to 535, as said below
Outputs:
- grad_in: float32 [4096, 256], P('dom', 'query')
- grad_w: float32 [2, 64, 64], replicated
- grad_rel: float32 [2, 535, 64], replicated
Inputs may be any that keep to these rules, and one draw needn't show every extreme that they name: `edges_in`: row 0 is a local source row, row 1 a local destination row, row 2 a relation; relation 535 marks padding, which follows all real edges in each partition's block of 1024; at least a quarter of each block is real and some partition's block has no padding. `edges_bd`: row 0 is a ghost index below 256, row 1 a local destination row, row 2 a relation; relation 535 marks padding, which follows all real edges in each partition's block of 1024; at least a quarter of each block is real and some partition's block has no padding.
All inputs are finite; a program needn't handle non-finite values.
Results may differ from a plain program's by a relative error of at most 0.0049.
The roundings to bfloat16 on the way count: a program that leaves them out, or rounds other values in their place, can miss the bound.
Values may be sent and summed in bfloat16 or wider, within the bound.
A program may use at most 64 MiB of HBM per device.

v0:
```python
import functools
import math

import jax
import jax.numpy as jnp
from jax import lax
from jax.experimental import pallas as pl
from jax.experimental.pallas import tpu as pltpu
from jax.sharding import PartitionSpec as P

MESH = pl.DeviceIdType.MESH
F32 = jnp.float32
BF16 = jnp.bfloat16
CHUNK = 16


def dot_nn(a, b):
    return lax.dot_general(a, b, (((1,), (0,)), ((), ())), preferred_element_type=F32)


def dot_nt(a, b):
    return lax.dot_general(a, b, (((1,), (1,)), ((), ())), preferred_element_type=F32)


def split_hi_lo(x, axis):
    hi = x.astype(BF16)
    lo = (x - hi.astype(F32)).astype(BF16)
    return jnp.concatenate([hi, lo], axis=axis)


def onehot_into(dest, ids, col0, block):
    rows = dest.shape[0]
    count = ids.shape[1]

    def fill(i, carry):
        base = pl.multiple_of(i * block, block)
        row_ids = lax.broadcasted_iota(jnp.int32, (block, count), 0) + base
        dest[pl.ds(base, block), pl.ds(col0, count)] = jnp.where(row_ids == ids, 1.0, 0.0).astype(BF16)
        return carry

    lax.fori_loop(0, rows // block, fill, 0)


def loop(low, high, step):
    if high - low <= 32:
        for i in range(low, high):
            step(i, 0)
    else:
        lax.fori_loop(low, high, step, 0)


def div(a, b):
    return a // b if isinstance(a, int) else lax.div(a, b)


def rem(a, b):
    return a % b if isinstance(a, int) else lax.rem(a, b)


def aligned(a, b):
    return a if isinstance(a, int) else pl.multiple_of(a, b)


def kernel(
    n_q,
    n_d,
    scale_w,
    scale_r,
    rel_count,
    rel_rows,
    *refs,
):
    n_in = 13
    hbm = refs[:n_in]
    gin_ref, gw_ref, grel_ref = refs[n_in : n_in + 3]
    local = refs[n_in + 3 : 2 * n_in + 3]
    (
        h_ref, cot_ref, w1_ref, w2_ref, r1_ref, r2_ref, qe_ref, qhead_ref, qrel_ref, bnd_ref, gs_ref, ein_ref, ebd_ref,
    ) = local
    (
    relt,
    gs_x,
    rt,
    vt,
    st_in,
    st_bd,
    rel_e,
    x1,
    x2,
    req,
    out1,
    ghost1,
    out2,
    ghost2,
    ret_out2,
    ret_in2,
    ret_out1,
    ret_in1,
    red_src,
    red_in,
    red_sum,
    red_all,
    xsend,
    xrecv,
    rsend,
    rrecv,
    gsend,
    grecv,
    load_sem,
    ) = refs[2 * n_in + 3 :]
    me_d = lax.axis_index("dom")
    me_q = lax.axis_index("query")
    total = n_q * n_d
    lin = me_q * n_d + me_d
    feat = w1_ref.shape[0]
    rows, wide = h_ref.shape
    queries = wide // feat
    send = ghost1.shape[0] // n_d
    e_in = ein_ref.shape[1]
    e_bd = ebd_ref.shape[1]
    lanes = red_all.shape[2] // 128
    n_chunks = feat // CHUNK * lanes

    def tile_of(c):
        return (
            pl.ds(aligned(div(c, lanes) * CHUNK, CHUNK), CHUNK),
            pl.ds(aligned(rem(c, lanes) * 128, 128), 128),
        )

    barrier = pltpu.get_barrier_semaphore()

    def greet(i, carry):
        t = lax.rem(lin + i, total)
        pl.semaphore_signal(
            barrier, inc=1, device_id=(div(t, n_d), rem(t, n_d)), device_id_type=MESH
        )
        return carry

    loop(1, total, greet)
    loads = [
        pltpu.make_async_copy(src, dst, load_sem.at[k])
        for k, (src, dst) in enumerate(zip(hbm, local))
    ]
    for load in loads:
        load.start()
    for load in loads:
        load.wait()

    def block_copy(phase, src, dst, size, i, send_to):
        peer = lax.rem(me_d + i, n_d)
        del send_to
        if size is None:
            s, d = src.at[peer], dst.at[me_d]
        else:
            s = src.at[pl.ds(pl.multiple_of(peer * size, size), size)]
            d = dst.at[pl.ds(pl.multiple_of(me_d * size, size), size)]
        return pltpu.make_async_remote_copy(
            src_ref=s,
            dst_ref=d,
            send_sem=xsend.at[phase, i],
            recv_sem=xrecv.at[phase, i],
            device_id=(me_q, peer),
            device_id_type=MESH,
        )

    def exchange_start(phase, src, dst, size):
        def go(i, carry):
            block_copy(phase, src, dst, size, i, True).start()
            return carry

        loop(1, n_d, go)
        if size is None:
            dst[me_d] = src[me_d]
        else:
            own = pl.ds(pl.multiple_of(me_d * size, size), size)
            dst[own, :] = src[own, :]

    def exchange_wait(phase, src, dst, size):
        def go(i, carry):
            block_copy(phase, src, dst, size, i, False).wait()
            return carry

        loop(1, n_d, go)

    mine = (lin * n_chunks + total - 1) // total
    adds = jnp.logical_and(mine < n_chunks, (mine * total) // n_chunks == lin)

    def rs_copy(layer, c):
        t = div(c * total, n_chunks)
        return t, pltpu.make_async_remote_copy(
            src_ref=red_src.at[(layer, *tile_of(c))],
            dst_ref=red_in.at[layer, lin],
            send_sem=rsend.at[layer, c],
            recv_sem=rrecv.at[layer, lin],
            device_id=(div(t, n_d), rem(t, n_d)),
            device_id_type=MESH,
        )

    def rs_start(layer):
        def go(c, carry):
            t, copy = rs_copy(layer, c)

            @pl.when(t != lin)
            def _():
                copy.start()

            return carry

        loop(0, n_chunks, go)

    def ag_copy(layer, c, i):
        t = lax.rem(lin + i, total)
        return pltpu.make_async_remote_copy(
            src_ref=red_sum.at[layer],
            dst_ref=red_all.at[(layer, *tile_of(c))],
            send_sem=gsend.at[layer, i],
            recv_sem=grecv.at[layer, c],
            device_id=(div(t, n_d), rem(t, n_d)),
            device_id_type=MESH,
        )

    def rs_finish_ag_start(layer):
        @pl.when(adds)
        def _():
            def take(i, carry):
                s = lax.rem(lin + i, total)
                pltpu.make_async_remote_copy(
                    src_ref=red_src.at[(layer, *tile_of(0))],
                    dst_ref=red_in.at[layer, s],
                    send_sem=rsend.at[layer, 0],
                    recv_sem=rrecv.at[layer, s],
                    device_id=(div(s, n_d), rem(s, n_d)),
                    device_id_type=MESH,
                ).wait_recv()
                return carry

            loop(1, total, take)
            red_in[layer, lin] = red_src[(layer, *tile_of(mine))]
            acc = jnp.sum(red_in[layer].astype(F32), axis=0).astype(BF16)
            red_sum[layer] = acc
            red_all[(layer, *tile_of(mine))] = acc

            def put(i, carry):
                ag_copy(layer, mine, i).start()
                return carry

            loop(1, total, put)

    def ag_finish(layer):
        def each(c, carry):
            t, copy = rs_copy(layer, c)

            @pl.when(t != lin)
            def _():
                copy.wait_send()
                ag_copy(layer, c, 1).wait_recv()

            return carry

        loop(0, n_chunks, each)

        @pl.when(adds)
        def _():
            def done(i, carry):
                ag_copy(layer, mine, i).wait_send()
                return carry

            loop(1, total, done)

    def pack(layer, rg, wg):
        parts = [rg, wg]
        left = lanes * 128 - rel_rows - feat
        if left:
            parts.append(jnp.zeros((feat, left), F32))
        red_src[layer] = jnp.concatenate(parts, axis=1).astype(BF16)

    def unpack(layer):
        summed = red_all[layer].astype(F32)
        grel_ref[layer] = summed[:, :rel_count] * scale_r
        gw_ref[layer] = summed[:, rel_rows : rel_rows + feat] * scale_w

    per = 128 // send
    spread = jnp.concatenate([gs_ref[...]] * per, axis=1)
    for p in range(n_d):
        gs_x[p] = spread[p : p + 1, :]

    onehot_into(vt, ein_ref[1:2, :], 0, 64)
    onehot_into(vt, ebd_ref[1:2, :], e_in, 64)
    pl.semaphore_wait(barrier, total - 1)
    exchange_start(0, gs_x, req, None)
    onehot_into(st_in, ein_ref[0:1, :], 0, 64)
    onehot_into(st_bd, ebd_ref[0:1, :], 0, 64)
    onehot_into(rt, ein_ref[2:3, :], 0, 32)
    onehot_into(rt, ebd_ref[2:3, :], e_in, 32)
    relt[...] = jnp.zeros_like(relt)
    relt[pl.ds(0, feat), pl.ds(0, rel_count)] = r1_ref[...]
    relt[pl.ds(feat, feat), pl.ds(0, rel_count)] = r2_ref[...]
    rel_e[...] = dot_nn(relt[...], rt[...]).astype(BF16)

    row_ids = lax.broadcasted_iota(jnp.int32, (feat, rows), 1) + me_d * rows
    lane_rel = lax.broadcasted_iota(jnp.int32, (feat, rel_count), 1)
    qtab = qe_ref[...].astype(F32)
    boost_parts = []
    for q in range(queries):
        vec = jnp.sum(jnp.where(lane_rel == qrel_ref[q], qtab, 0.0), axis=1, keepdims=True)
        boost_parts.append(jnp.where(row_ids == qhead_ref[q], vec, 0.0))
    boost = jnp.concatenate(boost_parts, axis=0)

    exchange_wait(0, gs_x, req, None)
    lane_group = lax.broadcasted_iota(jnp.int32, (1, 128), 1) // send
    wanted = []
    for j in range(n_d // per):
        vec = jnp.zeros((1, 128), jnp.int32)
        for k in range(per):
            vec = jnp.where(lane_group == k, req[j * per + k, 0:1, :], vec)
        wanted.append(vec)
    wanted = jnp.concatenate(wanted, axis=1)
    slots = bnd_ref.shape[1]
    slot_ids = lax.broadcasted_iota(jnp.int32, (slots, n_d * send), 0)
    own_ids = lax.broadcasted_iota(jnp.int32, (rows, slots), 0)
    row_of = jnp.where(own_ids == bnd_ref[...], 1.0, 0.0).astype(BF16)
    pick_t32 = dot_nn(row_of, jnp.where(slot_ids == wanted, 1.0, 0.0).astype(BF16))
    pick_t = pick_t32.astype(BF16)
    pick = pick_t32.T.astype(BF16)

    out1[...] = dot_nn(pick, h_ref[...]).astype(BF16)
    exchange_start(1, out1, ghost1, send)

    h32 = h_ref[...].astype(F32)
    h_t32 = h32.T
    h_t = h_t32.astype(BF16)

    def rel_tile(layer, lo, count):
        part = rel_e[pl.ds(layer * feat, feat), pl.ds(lo, count)].astype(F32)
        return jnp.concatenate([part] * queries, axis=0)

    def aggregate(layer, table_t, onehot, save, lo, count):
        sourced = dot_nn(table_t, onehot[...])
        save[:, pl.ds(lo, count)] = sourced.astype(BF16)
        message = split_hi_lo(sourced * rel_tile(layer, lo, count), 0)
        both = dot_nt(message, vt[:, pl.ds(lo, count)])
        return both[:wide] + both[wide:]

    def normalise(summed, w_ref):
        summed_b = summed.astype(BF16)
        normed, rstds = [], []
        for q in range(queries):
            mixed = lax.dot_general(
                w_ref[...],
                summed_b[q * feat : (q + 1) * feat],
                (((0,), (0,)), ((), ())),
                preferred_element_type=F32,
            )
            center = mixed - jnp.mean(mixed, axis=0, keepdims=True)
            rstd = lax.rsqrt(jnp.mean(center * center, axis=0, keepdims=True) + 1e-05)
            normed.append(center * rstd)
            rstds.append(rstd)
        return summed_b, normed, rstds

    def back_layer(up_t, normed, rstds, summed_b, w_ref):
        wgrad = jnp.zeros((feat, feat), F32)
        dsum = []
        for q in range(queries):
            y = normed[q]
            sig = jax.nn.sigmoid(y)
            dact = up_t[q * feat : (q + 1) * feat] * sig * (1.0 + y * (1.0 - sig))
            dmix = rstds[q] * (
                dact
                - jnp.mean(dact, axis=0, keepdims=True)
                - y * jnp.mean(dact * y, axis=0, keepdims=True)
            )
            dmix_b = dmix.astype(BF16)
            wgrad = wgrad + dot_nt(summed_b[q * feat : (q + 1) * feat], dmix_b)
            dsum.append(dot_nn(w_ref[...], dmix_b).astype(BF16))
        return wgrad, jnp.concatenate(dsum, axis=0)

    def rel_grad(down, save):
        prod = down * save[...].astype(F32)
        tot = prod[:feat]
        for q in range(1, queries):
            tot = tot + prod[q * feat : (q + 1) * feat]
        both = dot_nt(split_hi_lo(tot, 0), rt[pl.ds(0, rel_rows), :])
        return both[:feat] + both[feat:]

    def table_grad(layer, down, onehot, lo, count):
        message = split_hi_lo(down[:, lo : lo + count] * rel_tile(layer, lo, count), 0)
        both = dot_nt(onehot[...], message)
        return both[:, :wide] + both[:, wide:]

    def give_back(ret_in):
        return dot_nn(pick_t, ret_in[...])

    sum1 = aggregate(0, h_t, st_in, x1, 0, e_in) + boost
    exchange_wait(1, out1, ghost1, send)
    sum1 = sum1 + aggregate(0, ghost1[...].astype(F32).T.astype(BF16), st_bd, x1, e_in, e_bd)
    sum1_b, norm1, rstd1 = normalise(sum1, w1_ref)
    h2_t = (
        jnp.concatenate([y * jax.nn.sigmoid(y) for y in norm1], axis=0) + h_t32
    ).astype(BF16)

    out2[...] = dot_nt(pick, h2_t).astype(BF16)
    exchange_start(2, out2, ghost2, send)
    sum2 = aggregate(1, h2_t, st_in, x2, 0, e_in) + boost
    exchange_wait(2, out2, ghost2, send)
    sum2 = sum2 + aggregate(1, ghost2[...].astype(F32).T.astype(BF16), st_bd, x2, e_in, e_bd)
    sum2_b, norm2, rstd2 = normalise(sum2, w2_ref)

    cot32 = cot_ref[...].astype(F32)
    wg2, dsum2 = back_layer(cot32.T, norm2, rstd2, sum2_b, w2_ref)
    down2 = dot_nn(dsum2, vt[...])
    ret_out2[...] = table_grad(1, down2, st_bd, e_in, e_bd).astype(BF16)
    exchange_start(3, ret_out2, ret_in2, send)
    mid = cot32 + table_grad(1, down2, st_in, 0, e_in)
    pack(1, rel_grad(down2, x2), wg2)
    exchange_wait(3, ret_out2, ret_in2, send)
    rs_start(1)
    mid = mid + give_back(ret_in2)

    wg1, dsum1 = back_layer(mid.T, norm1, rstd1, sum1_b, w1_ref)
    down1 = dot_nn(dsum1, vt[...])
    pack(0, rel_grad(down1, x1), wg1)
    rs_start(0)
    ret_out1[...] = table_grad(0, down1, st_bd, e_in, e_bd).astype(BF16)
    exchange_start(4, ret_out1, ret_in1, send)
    rs_finish_ag_start(1)
    base = mid + table_grad(0, down1, st_in, 0, e_in)
    rs_finish_ag_start(0)
    exchange_wait(4, ret_out1, ret_in1, send)
    gin_ref[...] = base + give_back(ret_in1)
    ag_finish(1)
    unpack(1)
    ag_finish(0)
    unpack(0)


def body(
    h_in,
    cotangent,
    w_one,
    w_two,
    rel_one,
    rel_two,
    query_emb,
    q_head,
    q_rel,
    bnd_rows,
    ghost_slots,
    edges_in,
    edges_bd,
):
    rows, wide = h_in.shape
    feat = w_one.shape[0]
    queries = wide // feat
    rel_count = rel_one.shape[0]
    n_d = lax.axis_size("dom")
    n_q = lax.axis_size("query")
    total = n_d * n_q
    send = ghost_slots.shape[1]
    ghosts = n_d * send
    e_in, e_bd = edges_in.shape[1], edges_bd.shape[1]
    edges = e_in + e_bd
    rel_pad = -(-(rel_count + 1) // 128) * 128
    rel_rows = -(-(rel_count + 1) // 16) * 16
    width = -(-(rel_rows + feat) // 128) * 128
    n_chunks = feat // CHUNK * (width // 128)
    scale_w = 1.0 / math.sqrt(rows * n_d * queries * n_q)
    scale_r = math.sqrt(rel_count / (n_d * edges * queries * n_q))

    args = (
        h_in,
        cotangent,
        w_one,
        w_two,
        rel_one.T,
        rel_two.T,
        query_emb.T,
        q_head,
        q_rel,
        bnd_rows[None, :],
        ghost_slots,
        edges_in,
        edges_bd,
    )
    spaces = [pltpu.VMEM] * 7 + [pltpu.SMEM] * 2 + [pltpu.VMEM] * 4

    vmem = pl.BlockSpec(memory_space=pltpu.VMEM)
    dma = pltpu.SemaphoreType.DMA
    grad_in, grad_w, grad_rel_t = pl.pallas_call(
        functools.partial(kernel, n_q, n_d, scale_w, scale_r, rel_count, rel_rows),
        out_shape=(
            jax.ShapeDtypeStruct((rows, wide), F32),
            jax.ShapeDtypeStruct((2, feat, feat), F32),
            jax.ShapeDtypeStruct((2, feat, rel_count), F32),
        ),
        in_specs=[pl.BlockSpec(memory_space=pltpu.HBM)] * len(args),
        out_specs=(vmem, vmem, vmem),
        scratch_shapes=[
            *(space(a.shape, a.dtype) for a, space in zip(args, spaces)),
            pltpu.VMEM((2 * feat, rel_pad), BF16),
            pltpu.VMEM((n_d, 1, 128), jnp.int32),
            pltpu.VMEM((rel_pad, edges), BF16),
            pltpu.VMEM((rows, edges), BF16),
            pltpu.VMEM((rows, e_in), BF16),
            pltpu.VMEM((ghosts, e_bd), BF16),
            pltpu.VMEM((2 * feat, edges), BF16),
            pltpu.VMEM((wide, edges), BF16),
            pltpu.VMEM((wide, edges), BF16),
            pltpu.VMEM((n_d, 1, 128), jnp.int32),
            pltpu.VMEM((ghosts, wide), BF16),
            pltpu.VMEM((ghosts, wide), BF16),
            pltpu.VMEM((ghosts, wide), BF16),
            pltpu.VMEM((ghosts, wide), BF16),
            pltpu.VMEM((ghosts, wide), BF16),
            pltpu.VMEM((ghosts, wide), BF16),
            pltpu.VMEM((ghosts, wide), BF16),
            pltpu.VMEM((ghosts, wide), BF16),
            pltpu.VMEM((2, feat, width), BF16),
            pltpu.VMEM((2, total, CHUNK, 128), BF16),
            pltpu.VMEM((2, CHUNK, 128), BF16),
            pltpu.VMEM((2, feat, width), BF16),
            dma((5, n_d)),
            dma((5, n_d)),
            dma((2, n_chunks)),
            dma((2, total)),
            dma((2, total)),
            dma((2, n_chunks)),
            dma((len(args),)),
        ],
        compiler_params=pltpu.CompilerParams(
            collective_id=0, has_side_effects=True, vmem_limit_bytes=67043328
        ),
    )(*args)
    return grad_in, grad_w, jnp.swapaxes(grad_rel_t, 1, 2)


def solution(mesh):
    return jax.shard_map(
        body,
        mesh=mesh,
        in_specs=(
            P("dom", "query"),
            P("dom", "query"),
            P(),
            P(),
            P(),
            P(),
            P(),
            P("query"),
            P("query"),
            P("dom"),
            P("dom", None),
            P(None, "dom"),
            P(None, "dom"),
        ),
        out_specs=(P("dom", "query"), P(), P()),
        check_vma=False,
    )
```

profile of v0, /device:TPU:0, one launch (start us, length us, event | category | flops | bytes accessed | tf_op | source)
XLA Modules:
  0.0 47.3 jit_solution(14628201023702797645)
XLA Ops:
  0.6 42.8 %shard_map.148 = (f32[256,128]{1,0:T(8,128)}, f32[2,64,64]{2,1,0:T(8,128)}, f32[2,64,535]{2,1,0:T(8,128)}) custom-call(bf16[256,128]{1,0:T(8,128)(2,1)} %refs_0_.1, bf16[256,128]{1,0:T(8,128)(2,1)} %refs_1_.1, bf16[64,64]{1,0:T(8,128)(2,1)} %refs_2_.1, bf16[64,64]{1,0:T(8,128)(2,1)} %refs_3_.1, bf16[64,535]{1,0:T(8,128)(2,1)} %bitcast.6, ...), custom_call_target="tpu_custom_call" | custom-call | tf_op jit(solution)/shard_map/pallas_call | solution.py:488
  43.4 0.0 copy-start
  43.4 1.6 %copy.19 = f32[256,128]{1,0:T(8,128)} copy(f32[256,128]{1,0:T(8,128)} %get-tuple-element.12) | data formatting | bytes 262144
  45.1 1.5 %copy.20 = f32[2,64,64]{2,1,0:T(8,128)} copy(f32[2,64,64]{2,1,0:T(8,128)} %get-tuple-element.13) | data formatting | bytes 65536
  46.5 0.0 copy-done
  46.5 0.7 %copy.21 = f32[2,535,64]{1,2,0:T(8,128)} copy(f32[2,535,64]{1,2,0:T(8,128)S(1)} %bitcast.5) | data formatting | bytes 547840
Async XLA Ops:
  43.4 3.1 %copy-start = (f32[2,64,535]{2,1,0:T(8,128)S(1)}, f32[2,64,535]{2,1,0:T(8,128)}, u32[]{:S(2)}) copy-start(f32[2,64,535]{2,1,0:T(8,128)} %get-tuple-element.8) | copy-start | bytes 821764
where the time goes:
time: 47.5 us; the launch traced here: 47.3 us
  Pallas kernels  42.8 us (90%)
  local copies, waits for them, and re-layouts  3.81 us (8%)
  between operations  0.65 us (1%)
    pallas_call x1, Pallas kernels, body(): pl.pallas_call(functools.partial(kernel, n_q, n_d, scale_w, scale_r, rel_...  42.8 us
    unnamed x5, local copies, waits for them, and re-layouts  3.81 us

commit v1 on v0

v1 whole, which is shorter than its diff:
```python
import functools
import math

import jax
import jax.numpy as jnp
from jax import lax
from jax.experimental import pallas as pl
from jax.experimental.pallas import tpu as pltpu
from jax.sharding import PartitionSpec as P

MESH = pl.DeviceIdType.MESH
F32 = jnp.float32
BF16 = jnp.bfloat16
RS_EARLY = False


def dot_nn(a, b):
    return lax.dot_general(a, b, (((1,), (0,)), ((), ())), preferred_element_type=F32)


def dot_nt(a, b):
    return lax.dot_general(a, b, (((1,), (1,)), ((), ())), preferred_element_type=F32)


def split_hi_lo(x, axis):
    hi = x.astype(BF16)
    lo = (x - hi.astype(F32)).astype(BF16)
    return jnp.concatenate([hi, lo], axis=axis)


def onehot_into(dest, ids, col0, block):
    rows = dest.shape[0]
    count = ids.shape[1]

    def fill(i, carry):
        base = pl.multiple_of(i * block, block)
        row_ids = lax.broadcasted_iota(jnp.int32, (block, count), 0) + base
        dest[pl.ds(base, block), pl.ds(col0, count)] = jnp.where(row_ids == ids, 1.0, 0.0).astype(BF16)
        return carry

    lax.fori_loop(0, rows // block, fill, 0)


def loop(low, high, step):
    if high - low <= 32:
        for i in range(low, high):
            step(i, 0)
    else:
        lax.fori_loop(low, high, step, 0)


def div(a, b):
    return a // b if isinstance(a, int) else lax.div(a, b)


def rem(a, b):
    return a % b if isinstance(a, int) else lax.rem(a, b)


def aligned(a, b):
    return a if isinstance(a, int) else pl.multiple_of(a, b)


def kernel(
    n_q,
    n_d,
    grp,
    scale_w,
    scale_r,
    rel_count,
    rel_rows,
    *refs,
):
    n_in = 13
    hbm = refs[:n_in]
    gin_ref, gw_ref, grel_ref = refs[n_in : n_in + 3]
    local = refs[n_in + 3 : 2 * n_in + 3]
    (
        h_ref, cot_ref, w1_ref, w2_ref, r1_ref, r2_ref, qe_ref, qhead_ref, qrel_ref, bnd_ref, gs_ref, ein_ref, ebd_ref,
    ) = local
    (
    relt,
    gs_x,
    rt,
    vt,
    st_in,
    st_bd,
    rel_e,
    x1,
    x2,
    req,
    out1,
    ghost1,
    out2,
    ghost2,
    ret_out2,
    ret_in2,
    ret_out1,
    ret_in1,
    red_src,
    red_in,
    red_z,
    red_all,
    xsend,
    xrecv,
    asend,
    arecv,
    load_sem,
    ) = refs[2 * n_in + 3 :]
    me_d = lax.axis_index("dom")
    me_q = lax.axis_index("query")
    n_far = n_d // grp
    n_near = n_q * grp
    far = lax.div(me_d, grp)
    near = lax.rem(me_d, grp)
    me_n = me_q * grp + near
    feat = w1_ref.shape[0]
    rows, wide = h_ref.shape
    queries = wide // feat
    send = ghost1.shape[0] // n_d
    e_in = ein_ref.shape[1]
    e_bd = ebd_ref.shape[1]
    width = red_src.shape[3]

    barrier = pltpu.get_barrier_semaphore()

    def greet(i, carry):
        t = lax.rem(me_d + i, n_d)
        pl.semaphore_signal(barrier, inc=1, device_id=(me_q, t), device_id_type=MESH)
        return carry

    loop(1, n_d, greet)
    for dq in range(1, n_q):
        for k in range(grp):
            pl.semaphore_signal(
                barrier,
                inc=1,
                device_id=(lax.rem(me_q + dq, n_q), far * grp + k),
                device_id_type=MESH,
            )
    greeted = n_d - 1 + (n_q - 1) * grp
    loads = [
        pltpu.make_async_copy(src, dst, load_sem.at[k])
        for k, (src, dst) in enumerate(zip(hbm, local))
    ]
    for load in loads[::-1]:
        load.start()
    for load in loads[::-1]:
        load.wait()

    def peer_loop(step):
        if n_d <= 32:
            order = sorted(range(1, n_d), key=lambda i: -min(i // grp, n_far - i // grp))
            for i in order:
                step(i, 0)
        else:
            lax.fori_loop(1, n_d, step, 0)

    def exchange_start(phase, src, dst, size):
        def go(i, carry):
            peer = lax.rem(me_d + i, n_d)
            if size is None:
                s, d = src.at[peer], dst.at[me_d]
            else:
                s = src.at[pl.ds(pl.multiple_of(peer * size, size), size)]
                d = dst.at[pl.ds(pl.multiple_of(me_d * size, size), size)]
            pltpu.make_async_remote_copy(
                src_ref=s,
                dst_ref=d,
                send_sem=xsend.at[phase],
                recv_sem=xrecv.at[phase],
                device_id=(me_q, peer),
                device_id_type=MESH,
            ).start()
            return carry

        peer_loop(go)
        if size is None:
            dst[me_d] = src[me_d]
        else:
            own = pl.ds(pl.multiple_of(me_d * size, size), size)
            dst[own, :] = src[own, :]

    def exchange_wait(phase, src, dst, size):
        some = pl.ds(0, (n_d - 1) * (size or 1))
        pltpu.make_async_remote_copy(
            src_ref=src.at[some],
            dst_ref=dst.at[some],
            send_sem=xsend.at[phase],
            recv_sem=xrecv.at[phase],
            device_id=(me_q, lax.rem(me_d + 1, n_d)),
            device_id_type=MESH,
        ).wait()

    def near_device(t):
        return lax.div(t, grp), far * grp + lax.rem(t, grp)

    def all_copy(layer, stage, src, dst, device):
        return pltpu.make_async_remote_copy(
            src_ref=src,
            dst_ref=dst,
            send_sem=asend.at[layer, stage],
            recv_sem=arecv.at[layer, stage],
            device_id=device,
            device_id_type=MESH,
        )

    def scatter_start(layer):
        def go(j, carry):
            t = lax.rem(me_n + j, n_near)
            all_copy(layer, 0, red_src.at[layer, t], red_in.at[layer, me_n], near_device(t)).start()
            return carry

        loop(1, n_near, go)

    def far_start(layer):
        some = pl.ds(0, n_near - 1)
        all_copy(
            layer, 0, red_src.at[layer, some], red_in.at[layer, some], near_device(lax.rem(me_n + 1, n_near))
        ).wait()
        red_in[layer, me_n] = red_src[layer, me_n]
        red_z[layer, far] = jnp.sum(red_in[layer].astype(F32), axis=0).astype(BF16)

        def go(j, carry):
            t = lax.rem(far + j, n_far)
            all_copy(layer, 1, red_z.at[layer, far], red_z.at[layer, far], (me_q, t * grp + near)).start()
            return carry

        loop(1, n_far, go)

    def gather_start(layer):
        if n_far > 1:
            some = pl.ds(0, n_far - 1)
            all_copy(
                layer,
                1,
                red_z.at[layer, some],
                red_z.at[layer, some],
                (me_q, lax.rem(far + 1, n_far) * grp + near),
            ).wait()
        red_all[layer, me_n] = jnp.sum(red_z[layer].astype(F32), axis=0).astype(BF16)

        def go(j, carry):
            t = lax.rem(me_n + j, n_near)
            all_copy(layer, 2, red_all.at[layer, me_n], red_all.at[layer, me_n], near_device(t)).start()
            return carry

        loop(1, n_near, go)

    def gather_wait(layer):
        some = pl.ds(0, n_near - 1)
        all_copy(
            layer, 2, red_all.at[layer, some], red_all.at[layer, some], near_device(lax.rem(me_n + 1, n_near))
        ).wait()

    def pack(layer, rg, wg):
        parts = [rg, wg]
        left = width - rel_rows - feat
        if left:
            parts.append(jnp.zeros((feat, left), F32))
        whole = jnp.concatenate(parts, axis=1)
        red_src[layer] = whole.reshape(n_near, feat // n_near, width).astype(BF16)

    def unpack(layer):
        summed = red_all[layer].astype(F32).reshape(feat, width)
        grel_ref[layer] = summed[:, :rel_count] * scale_r
        gw_ref[layer] = summed[:, rel_rows : rel_rows + feat] * scale_w

    per = 128 // send
    spread = jnp.concatenate([gs_ref[...]] * per, axis=1)
    for p in range(n_d):
        gs_x[p] = spread[p : p + 1, :]

    onehot_into(vt, ein_ref[1:2, :], 0, 64)
    onehot_into(vt, ebd_ref[1:2, :], e_in, 64)
    pl.semaphore_wait(barrier, greeted)
    exchange_start(0, gs_x, req, None)
    onehot_into(st_in, ein_ref[0:1, :], 0, 64)
    onehot_into(st_bd, ebd_ref[0:1, :], 0, 64)

    slots = bnd_ref.shape[1]
    own_ids = lax.broadcasted_iota(jnp.int32, (rows, slots), 0)
    row_of32 = jnp.where(own_ids == bnd_ref[...], 1.0, 0.0)
    row_of = row_of32.astype(BF16)
    published = dot_nn(row_of32.T.astype(BF16), h_ref[...]).astype(BF16)

    exchange_wait(0, gs_x, req, None)
    lane_group = lax.broadcasted_iota(jnp.int32, (1, 128), 1) // send
    wanted = []
    for j in range(n_d // per):
        vec = jnp.zeros((1, 128), jnp.int32)
        for k in range(per):
            vec = jnp.where(lane_group == k, req[j * per + k, 0:1, :], vec)
        wanted.append(vec)
    wanted = jnp.concatenate(wanted, axis=1)
    slot_ids = lax.broadcasted_iota(jnp.int32, (slots, n_d * send), 0)
    slot_of32 = jnp.where(slot_ids == wanted, 1.0, 0.0)
    slot_of_t = slot_of32.T.astype(BF16)
    out1[...] = dot_nn(slot_of_t, published).astype(BF16)
    exchange_start(1, out1, ghost1, send)

    onehot_into(rt, ein_ref[2:3, :], 0, 32)
    onehot_into(rt, ebd_ref[2:3, :], e_in, 32)
    relt[...] = jnp.zeros_like(relt)
    relt[pl.ds(0, feat), pl.ds(0, rel_count)] = r1_ref[...]
    relt[pl.ds(feat, feat), pl.ds(0, rel_count)] = r2_ref[...]
    rel_e[...] = dot_nn(relt[...], rt[...]).astype(BF16)
    pick_t = dot_nn(row_of, slot_of32.astype(BF16)).astype(BF16)
    pick = dot_nt(slot_of_t, row_of).astype(BF16)

    row_ids = lax.broadcasted_iota(jnp.int32, (feat, rows), 1) + me_d * rows
    lane_rel = lax.broadcasted_iota(jnp.int32, (feat, rel_count), 1)
    qtab = qe_ref[...].astype(F32)
    boost_parts = []
    for q in range(queries):
        vec = jnp.sum(jnp.where(lane_rel == qrel_ref[q], qtab, 0.0), axis=1, keepdims=True)
        boost_parts.append(jnp.where(row_ids == qhead_ref[q], vec, 0.0))
    boost = jnp.concatenate(boost_parts, axis=0)

    h32 = h_ref[...].astype(F32)
    h_t32 = h32.T
    h_t = h_t32.astype(BF16)

    def rel_tile(layer, lo, count):
        part = rel_e[pl.ds(layer * feat, feat), pl.ds(lo, count)].astype(F32)
        return jnp.concatenate([part] * queries, axis=0)

    def aggregate(layer, table_t, onehot, save, lo, count):
        sourced = dot_nn(table_t, onehot[...])
        save[:, pl.ds(lo, count)] = sourced.astype(BF16)
        message = split_hi_lo(sourced * rel_tile(layer, lo, count), 0)
        both = dot_nt(message, vt[:, pl.ds(lo, count)])
        return both[:wide] + both[wide:]

    def normalise(summed, w_ref):
        summed_b = summed.astype(BF16)
        normed, rstds = [], []
        for q in range(queries):
            mixed = lax.dot_general(
                w_ref[...],
                summed_b[q * feat : (q + 1) * feat],
                (((0,), (0,)), ((), ())),
                preferred_element_type=F32,
            )
            center = mixed - jnp.mean(mixed, axis=0, keepdims=True)
            rstd = lax.rsqrt(jnp.mean(center * center, axis=0, keepdims=True) + 1e-05)
            normed.append(center * rstd)
            rstds.append(rstd)
        return summed_b, normed, rstds

    def back_layer(up_t, normed, rstds, summed_b, w_ref):
        wgrad = jnp.zeros((feat, feat), F32)
        dsum = []
        for q in range(queries):
            y = normed[q]
            sig = jax.nn.sigmoid(y)
            dact = up_t[q * feat : (q + 1) * feat] * sig * (1.0 + y * (1.0 - sig))
            dmix = rstds[q] * (
                dact
                - jnp.mean(dact, axis=0, keepdims=True)
                - y * jnp.mean(dact * y, axis=0, keepdims=True)
            )
            dmix_b = dmix.astype(BF16)
            wgrad = wgrad + dot_nt(summed_b[q * feat : (q + 1) * feat], dmix_b)
            dsum.append(dot_nn(w_ref[...], dmix_b).astype(BF16))
        return wgrad, jnp.concatenate(dsum, axis=0)

    def rel_grad(downs, save):
        tots = []
        lo = 0
        for down in downs:
            count = down.shape[1]
            prod = down * save[:, pl.ds(lo, count)].astype(F32)
            tot = prod[:feat]
            for q in range(1, queries):
                tot = tot + prod[q * feat : (q + 1) * feat]
            tots.append(split_hi_lo(tot, 0))
            lo += count
        both = dot_nt(jnp.concatenate(tots, axis=1), rt[pl.ds(0, rel_rows), :])
        return both[:feat] + both[feat:]

    def table_grad(layer, down, onehot, lo, count):
        message = split_hi_lo(down * rel_tile(layer, lo, count), 0)
        both = dot_nt(onehot[...], message)
        return both[:, :wide] + both[:, wide:]

    def give_back(ret_in):
        return dot_nn(pick_t, ret_in[...])

    sum1 = aggregate(0, h_t, st_in, x1, 0, e_in) + boost
    exchange_wait(1, out1, ghost1, send)
    sum1 = sum1 + aggregate(0, ghost1[...].astype(F32).T.astype(BF16), st_bd, x1, e_in, e_bd)
    sum1_b, norm1, rstd1 = normalise(sum1, w1_ref)
    h2_t = (
        jnp.concatenate([y * jax.nn.sigmoid(y) for y in norm1], axis=0) + h_t32
    ).astype(BF16)

    out2[...] = dot_nt(pick, h2_t).astype(BF16)
    exchange_start(2, out2, ghost2, send)
    sum2 = aggregate(1, h2_t, st_in, x2, 0, e_in) + boost
    exchange_wait(2, out2, ghost2, send)
    sum2 = sum2 + aggregate(1, ghost2[...].astype(F32).T.astype(BF16), st_bd, x2, e_in, e_bd)
    sum2_b, norm2, rstd2 = normalise(sum2, w2_ref)

    cot32 = cot_ref[...].astype(F32)
    wg2, dsum2 = back_layer(cot32.T, norm2, rstd2, sum2_b, w2_ref)
    down2_bd = dot_nn(dsum2, vt[:, pl.ds(e_in, e_bd)])
    ret_out2[...] = table_grad(1, down2_bd, st_bd, e_in, e_bd).astype(BF16)
    exchange_start(3, ret_out2, ret_in2, send)
    down2_in = dot_nn(dsum2, vt[:, pl.ds(0, e_in)])
    mid = cot32 + table_grad(1, down2_in, st_in, 0, e_in)
    pack(1, rel_grad((down2_in, down2_bd), x2), wg2)
    if RS_EARLY:
        scatter_start(1)
    exchange_wait(3, ret_out2, ret_in2, send)
    if not RS_EARLY:
        scatter_start(1)
    mid = mid + give_back(ret_in2)

    wg1, dsum1 = back_layer(mid.T, norm1, rstd1, sum1_b, w1_ref)
    down1_in = dot_nn(dsum1, vt[:, pl.ds(0, e_in)])
    down1_bd = dot_nn(dsum1, vt[:, pl.ds(e_in, e_bd)])
    pack(0, rel_grad((down1_in, down1_bd), x1), wg1)
    scatter_start(0)
    far_start(1)
    ret_out1[...] = table_grad(0, down1_bd, st_bd, e_in, e_bd).astype(BF16)
    exchange_start(4, ret_out1, ret_in1, send)
    base = mid + table_grad(0, down1_in, st_in, 0, e_in)
    far_start(0)
    gather_start(1)
    exchange_wait(4, ret_out1, ret_in1, send)
    gin_ref[...] = base + give_back(ret_in1)
    gather_start(0)
    gather_wait(1)
    unpack(1)
    gather_wait(0)
    unpack(0)


def write_out(*refs):
    half = (len(refs) - 1) // 2
    copies = [
        pltpu.make_async_copy(src, dst, refs[-1].at[k])
        for k, (src, dst) in enumerate(zip(refs[:half], refs[half : 2 * half]))
    ]
    for copy in copies:
        copy.start()
    for copy in copies:
        copy.wait()


def body(
    h_in,
    cotangent,
    w_one,
    w_two,
    rel_one,
    rel_two,
    query_emb,
    q_head,
    q_rel,
    bnd_rows,
    ghost_slots,
    edges_in,
    edges_bd,
):
    rows, wide = h_in.shape
    feat = w_one.shape[0]
    queries = wide // feat
    rel_count = rel_one.shape[0]
    n_d = lax.axis_size("dom")
    n_q = lax.axis_size("query")
    send = ghost_slots.shape[1]
    ghosts = n_d * send
    e_in, e_bd = edges_in.shape[1], edges_bd.shape[1]
    edges = e_in + e_bd
    rel_pad = -(-(rel_count + 1) // 128) * 128
    rel_rows = -(-(rel_count + 1) // 16) * 16
    width = -(-(rel_rows + feat) // 128) * 128
    grp = max(1, 8 // n_q)
    n_near, n_far = n_q * grp, n_d // grp
    part = feat // n_near
    scale_w = 1.0 / math.sqrt(rows * n_d * queries * n_q)
    scale_r = math.sqrt(rel_count / (n_d * edges * queries * n_q))

    args = (
        h_in,
        cotangent,
        w_one,
        w_two,
        rel_one.T,
        rel_two.T,
        query_emb.T,
        q_head,
        q_rel,
        bnd_rows[None, :],
        ghost_slots,
        edges_in,
        edges_bd,
    )
    spaces = [pltpu.VMEM] * 7 + [pltpu.SMEM] * 2 + [pltpu.VMEM] * 4

    vmem = pl.BlockSpec(memory_space=pltpu.VMEM)
    dma = pltpu.SemaphoreType.DMA
    shapes = (
        jax.ShapeDtypeStruct((rows, wide), F32),
        jax.ShapeDtypeStruct((2, feat, feat), F32),
        jax.ShapeDtypeStruct((2, feat, rel_count), F32),
    )
    results = pl.pallas_call(
        functools.partial(kernel, n_q, n_d, grp, scale_w, scale_r, rel_count, rel_rows),
        out_shape=shapes,
        in_specs=[pl.BlockSpec(memory_space=pltpu.HBM)] * len(args),
        out_specs=(vmem, vmem, vmem),
        scratch_shapes=[
            *(space(a.shape, a.dtype) for a, space in zip(args, spaces)),
            pltpu.VMEM((2 * feat, rel_pad), BF16),
            pltpu.VMEM((n_d, 1, 128), jnp.int32),
            pltpu.VMEM((rel_pad, edges), BF16),
            pltpu.VMEM((rows, edges), BF16),
            pltpu.VMEM((rows, e_in), BF16),
            pltpu.VMEM((ghosts, e_bd), BF16),
            pltpu.VMEM((2 * feat, edges), BF16),
            pltpu.VMEM((wide, edges), BF16),
            pltpu.VMEM((wide, edges), BF16),
            pltpu.VMEM((n_d, 1, 128), jnp.int32),
            pltpu.VMEM((ghosts, wide), BF16),
            pltpu.VMEM((ghosts, wide), BF16),
            pltpu.VMEM((ghosts, wide), BF16),
            pltpu.VMEM((ghosts, wide), BF16),
            pltpu.VMEM((ghosts, wide), BF16),
            pltpu.VMEM((ghosts, wide), BF16),
            pltpu.VMEM((ghosts, wide), BF16),
            pltpu.VMEM((ghosts, wide), BF16),
            pltpu.VMEM((2, n_near, part, width), BF16),
            pltpu.VMEM((2, n_near, part, width), BF16),
            pltpu.VMEM((2, n_far, part, width), BF16),
            pltpu.VMEM((2, n_near, part, width), BF16),
            dma((5,)),
            dma((5,)),
            dma((2, 3)),
            dma((2, 3)),
            dma((len(args),)),
        ],
        compiler_params=pltpu.CompilerParams(
            collective_id=0, has_side_effects=True, vmem_limit_bytes=33554432
        ),
    )(*args)
    grad_in, grad_w, grad_rel_t = pl.pallas_call(
        write_out,
        out_shape=shapes,
        in_specs=[vmem] * 3,
        out_specs=[pl.BlockSpec(memory_space=pltpu.HBM)] * 3,
        scratch_shapes=[dma((3,))],
    )(*results)
    return grad_in, grad_w, jnp.swapaxes(grad_rel_t, 1, 2)


def solution(mesh):
    return jax.shard_map(
        body,
        mesh=mesh,
        in_specs=(
            P("dom", "query"),
            P("dom", "query"),
            P(),
            P(),
            P(),
            P(),
            P(),
            P("query"),
            P("query"),
            P("dom"),
            P("dom", None),
            P(None, "dom"),
            P(None, "dom"),
        ),
        out_specs=(P("dom", "query"), P(), P()),
        check_vma=False,
    )
```

time: 47.5 us -> 51.1 us (1.076)
  local copies, waits for them, and re-layouts: 3.81 us -> 10.5 us
  Pallas kernels: 42.8 us -> 39.3 us
    unnamed x5 -> x32, local copies, waits for them, and re-layouts: 3.81 us -> 10.5 us
    pallas_call x1 -> x2, Pallas kernels: 42.8 us -> 39.3 us  [the longest x1 37.4 us: body(): pl.pallas_call(functools.partial(kernel, n_q, n_d, grp, scale_w, scale_r,...]
where the time goes in v1:
time: 51.1 us; the launch traced here: 50.5 us
  Pallas kernels  39.3 us (77%)
  local copies, waits for them, and re-layouts  10.5 us (21%)
  between operations  0.69 us (1%)
    pallas_call x1, Pallas kernels, body(): pl.pallas_call(functools.partial(kernel, n_q, n_d, grp, scale_w, scale_r,...  37.4 us
    unnamed x32, local copies, waits for them, and re-layouts  10.5 us
    pallas_call x1, Pallas kernels, body(): pl.pallas_call(write_out, out_shape=shapes, in_specs=[vmem] * 3, out_spec...  1.89 us

profile of v1, /device:TPU:0, one launch (start us, length us, event | category | flops | bytes accessed | tf_op | source)
XLA Modules:
  0.0 50.5 jit_solution(11310013162718938927)
XLA Ops:
  0.6 0.0 copy-start.13
  0.6 0.0 copy-start.14
  0.7 0.0 copy-start.15
  0.7 0.6 %copy-done.13 = s32[2]{0:T(128)S(1)} copy-done((s32[2]{0:T(128)S(1)}, s32[2]{0:T(128)}, u32[]{:S(2)}) %copy-start.13) | copy-done | bytes 32
  1.3 0.0 copy-done.14
  1.3 0.0 copy-done.15
  1.3 0.0 copy-start.2
  1.3 0.9 %copy-done.2 = bf16[535,64]{0,1:T(8,128)(2,1)S(1)} copy-done((bf16[535,64]{0,1:T(8,128)(2,1)S(1)}, bf16[535,64]{0,1:T(8,128)(2,1)}, u32[]{:S(2)}) %copy-start.2) | copy-done | bytes 68504
  2.2 0.0 copy-start.3
  2.2 0.9 %copy-done.3 = bf16[535,64]{0,1:T(8,128)(2,1)S(1)} copy-done((bf16[535,64]{0,1:T(8,128)(2,1)S(1)}, bf16[535,64]{0,1:T(8,128)(2,1)}, u32[]{:S(2)}) %copy-start.3) | copy-done | bytes 68504
  3.1 0.0 copy-start.4
  3.1 0.9 %copy-done.4 = bf16[535,64]{0,1:T(8,128)(2,1)S(1)} copy-done((bf16[535,64]{0,1:T(8,128)(2,1)S(1)}, bf16[535,64]{0,1:T(8,128)(2,1)}, u32[]{:S(2)}) %copy-start.4) | copy-done | bytes 68504
  4.0 0.0 copy-start.5
  4.0 0.8 %copy-done.5 = bf16[256,128]{1,0:T(8,128)(2,1)S(1)} copy-done((bf16[256,128]{1,0:T(8,128)(2,1)S(1)}, bf16[256,128]{1,0:T(8,128)(2,1)}, u32[]{:S(2)}) %copy-start.5) | copy-done | bytes 65560
  4.8 0.0 copy-start.6
  4.8 0.8 %copy-done.6 = bf16[256,128]{1,0:T(8,128)(2,1)S(1)} copy-done((bf16[256,128]{1,0:T(8,128)(2,1)S(1)}, bf16[256,128]{1,0:T(8,128)(2,1)}, u32[]{:S(2)}) %copy-start.6) | copy-done | bytes 65560
  5.7 0.0 copy-start.8
  5.7 0.7 %copy-done.8 = bf16[64,64]{1,0:T(8,128)(2,1)S(1)} copy-done((bf16[64,64]{1,0:T(8,128)(2,1)S(1)}, bf16[64,64]{1,0:T(8,128)(2,1)}, u32[]{:S(2)}) %copy-start.8) | copy-done | bytes 8216
  6.4 0.0 copy-start.9
  6.4 0.7 %copy-done.9 = bf16[64,64]{1,0:T(8,128)(2,1)S(1)} copy-done((bf16[64,64]{1,0:T(8,128)(2,1)S(1)}, bf16[64,64]{1,0:T(8,128)(2,1)}, u32[]{:S(2)}) %copy-start.9) | copy-done | bytes 8216
  7.1 0.0 copy-start.10
  7.1 0.7 %copy-done.10 = s32[3,1024]{1,0:T(4,128)S(1)} copy-done((s32[3,1024]{1,0:T(4,128)S(1)}, s32[3,1024]{1,0:T(4,128)}, u32[]{:S(2)}) %copy-start.10) | copy-done | bytes 12312
  7.8 0.0 copy-start.11
  7.8 0.7 %copy-done.11 = s32[3,1024]{1,0:T(4,128)S(1)} copy-done((s32[3,1024]{1,0:T(4,128)S(1)}, s32[3,1024]{1,0:T(4,128)}, u32[]{:S(2)}) %copy-start.11) | copy-done | bytes 12312
  8.5 0.0 copy-start.12
  8.5 0.7 %copy-done.12 = s32[16,16]{1,0:T(8,128)S(1)} copy-done((s32[16,16]{1,0:T(8,128)S(1)}, s32[16,16]{1,0:T(8,128)}, u32[]{:S(2)}) %copy-start.12) | copy-done | bytes 1048
  9.2 37.4 %shard_map.148 = (f32[256,128]{1,0:T(8,128)S(1)}, f32[2,64,64]{2,1,0:T(8,128)S(1)}, f32[2,64,535]{2,1,0:T(8,128)S(1)}) custom-call(bf16[256,128]{1,0:T(8,128)(2,1)S(1)} %copy-done.5, bf16[256,128]{1,0:T(8,128)(2,1)S(1)} %copy-done.6, bf16[64,64]{1,0:T(8,128)(2,1)S(1)} %copy-done.8, bf16[64,64]{1,0:T(8,128)(2,1)S(1)} %copy-done.9, ...), custom_call_target="tpu_custom_call" | custom-call | tf_op jit(solution)/shard_map/pallas_call | solution.py:510
  46.6 0.0 copy-start
  46.7 0.7 %copy-done = f32[2,64,535]{2,1,0:T(8,128)} copy-done((f32[2,64,535]{2,1,0:T(8,128)}, f32[2,64,535]{2,1,0:T(8,128)S(1)}, u32[]{:S(2)}) %copy-start) | copy-done | bytes 273944
  47.4 0.0 copy-start.1
  47.4 0.6 %copy-done.1 = f32[256,128]{1,0:T(8,128)} copy-done((f32[256,128]{1,0:T(8,128)}, f32[256,128]{1,0:T(8,128)S(1)}, u32[]{:S(2)}) %copy-start.1) | copy-done | bytes 131096
  48.0 0.0 copy-start.7
  48.0 0.6 %copy-done.7 = f32[2,64,64]{2,1,0:T(8,128)} copy-done((f32[2,64,64]{2,1,0:T(8,128)}, f32[2,64,64]{2,1,0:T(8,128)S(1)}, u32[]{:S(2)}) %copy-start.7) | copy-done | bytes 32792
  48.6 1.9 %shard_map.149 = (f32[256,128]{1,0:T(8,128)}, f32[2,64,64]{2,1,0:T(8,128)}, f32[2,64,535]{2,1,0:T(8,128)}) custom-call(f32[256,128]{1,0:T(8,128)} %copy-done.1, f32[2,64,64]{2,1,0:T(8,128)} %copy-done.7, f32[2,64,535]{2,1,0:T(8,128)} %copy-done), custom_call_target="tpu_custom_call" | custom-call | tf_op jit(solution)/shard_map/pallas_call | solution.py:549
Async XLA Ops:
  0.6 0.7 %copy-start.13 = (s32[2]{0:T(128)S(1)}, s32[2]{0:T(128)}, u32[]{:S(2)}) copy-start(s32[2]{0:T(128)} %refs_7_.1) | copy-start | bytes 28
  0.6 0.7 %copy-start.14 = (s32[2]{0:T(128)S(1)}, s32[2]{0:T(128)}, u32[]{:S(2)}) copy-start(s32[2]{0:T(128)} %refs_8_.1) | copy-start | bytes 28
  0.7 0.7 %copy-start.15 = (s32[64]{0:T(128)S(1)}, s32[64]{0:T(128)}, u32[]{:S(2)}) copy-start(s32[64]{0:T(128)} %param.22) | copy-start | bytes 772
  1.3 0.9 %copy-start.2 = (bf16[535,64]{0,1:T(8,128)(2,1)S(1)}, bf16[535,64]{0,1:T(8,128)(2,1)}, u32[]{:S(2)}) copy-start(bf16[535,64]{0,1:T(8,128)(2,1)} %param.17) | copy-start | bytes 205444
  2.2 0.9 %copy-start.3 = (bf16[535,64]{0,1:T(8,128)(2,1)S(1)}, bf16[535,64]{0,1:T(8,128)(2,1)}, u32[]{:S(2)}) copy-start(bf16[535,64]{0,1:T(8,128)(2,1)} %param.18) | copy-start | bytes 205444
  3.1 0.9 %copy-start.4 = (bf16[535,64]{0,1:T(8,128)(2,1)S(1)}, bf16[535,64]{0,1:T(8,128)(2,1)}, u32[]{:S(2)}) copy-start(bf16[535,64]{0,1:T(8,128)(2,1)} %param.19) | copy-start | bytes 205444
  4.0 0.8 %copy-start.5 = (bf16[256,128]{1,0:T(8,128)(2,1)S(1)}, bf16[256,128]{1,0:T(8,128)(2,1)}, u32[]{:S(2)}) copy-start(bf16[256,128]{1,0:T(8,128)(2,1)} %refs_0_.1) | copy-start | bytes 196612
  4.8 0.8 %copy-start.6 = (bf16[256,128]{1,0:T(8,128)(2,1)S(1)}, bf16[256,128]{1,0:T(8,128)(2,1)}, u32[]{:S(2)}) copy-start(bf16[256,128]{1,0:T(8,128)(2,1)} %refs_1_.1) | copy-start | bytes 196612
  5.7 0.7 %copy-start.8 = (bf16[64,64]{1,0:T(8,128)(2,1)S(1)}, bf16[64,64]{1,0:T(8,128)(2,1)}, u32[]{:S(2)}) copy-start(bf16[64,64]{1,0:T(8,128)(2,1)} %refs_2_.1) | copy-start | bytes 24580
  6.4 0.7 %copy-start.9 = (bf16[64,64]{1,0:T(8,128)(2,1)S(1)}, bf16[64,64]{1,0:T(8,128)(2,1)}, u32[]{:S(2)}) copy-start(bf16[64,64]{1,0:T(8,128)(2,1)} %refs_3_.1) | copy-start | bytes 24580
  7.1 0.7 %copy-start.10 = (s32[3,1024]{1,0:T(4,128)S(1)}, s32[3,1024]{1,0:T(4,128)}, u32[]{:S(2)}) copy-start(s32[3,1024]{1,0:T(4,128)} %refs_11_.1) | copy-start | bytes 36868
  7.8 0.7 %copy-start.11 = (s32[3,1024]{1,0:T(4,128)S(1)}, s32[3,1024]{1,0:T(4,128)}, u32[]{:S(2)}) copy-start(s32[3,1024]{1,0:T(4,128)} %refs_12_.1) | copy-start | bytes 36868
  8.5 0.7 %copy-start.12 = (s32[16,16]{1,0:T(8,128)S(1)}, s32[16,16]{1,0:T(8,128)}, u32[]{:S(2)}) copy-start(s32[16,16]{1,0:T(8,128)} %refs_10_.1) | copy-start | bytes 3076
  46.6 0.7 %copy-start = (f32[2,64,535]{2,1,0:T(8,128)}, f32[2,64,535]{2,1,0:T(8,128)S(1)}, u32[]{:S(2)}) copy-start(f32[2,64,535]{2,1,0:T(8,128)S(1)} %get-tuple-element.11.refs_2_) | copy-start | bytes 821764
  47.4 0.6 %copy-start.1 = (f32[256,128]{1,0:T(8,128)}, f32[256,128]{1,0:T(8,128)S(1)}, u32[]{:S(2)}) copy-start(f32[256,128]{1,0:T(8,128)S(1)} %get-tuple-element.9.refs_0_) | copy-start | bytes 393220
  48.0 0.6 %copy-start.7 = (f32[2,64,64]{2,1,0:T(8,128)}, f32[2,64,64]{2,1,0:T(8,128)S(1)}, u32[]{:S(2)}) copy-start(f32[2,64,64]{2,1,0:T(8,128)S(1)} %get-tuple-element.10.refs_1_) | copy-start | bytes 98308

commit v2 on v1

--- a/solution.py
+++ b/solution.py
@@ -509,7 +509,7 @@
     )
     results = pl.pallas_call(
         functools.partial(kernel, n_q, n_d, grp, scale_w, scale_r, rel_count, rel_rows),
-        out_shape=shapes,
+        out_shape=tuple(pltpu.VMEM(s.shape, s.dtype) for s in shapes),
         in_specs=[pl.BlockSpec(memory_space=pltpu.HBM)] * len(args),
         out_specs=(vmem, vmem, vmem),
         scratch_shapes=[
@@ -545,13 +545,14 @@
         compiler_params=pltpu.CompilerParams(
             collective_id=0, has_side_effects=True, vmem_limit_bytes=33554432
         ),
-    )(*args)
+    )(*(pltpu.with_memory_space_constraint(a, pltpu.HBM) for a in args))
     grad_in, grad_w, grad_rel_t = pl.pallas_call(
         write_out,
         out_shape=shapes,
         in_specs=[vmem] * 3,
         out_specs=[pl.BlockSpec(memory_space=pltpu.HBM)] * 3,
         scratch_shapes=[dma((3,))],
+        compiler_params=pltpu.CompilerParams(vmem_limit_bytes=16777216),
     )(*results)
     return grad_in, grad_w, jnp.swapaxes(grad_rel_t, 1, 2)
 

time: 51.1 us -> 39.2 us (0.77)
  local copies, waits for them, and re-layouts: 10.5 us -> 0 us
  Pallas kernels: 39.3 us -> 38.3 us
    unnamed x32 -> x0, local copies, waits for them, and re-layouts: 10.5 us -> none
    pallas_call x1, Pallas kernels: 1.89 us -> 0.82 us  [body(): pl.pallas_call(write_out, out_shape=shapes, in_specs=[vmem] * 3, out_spec...]
where the time goes in v2:
time: 39.2 us; the launch traced here: 39 us
  Pallas kernels  38.3 us (98%)
  between operations  0.64 us (2%)
    pallas_call x1, Pallas kernels, body(): pl.pallas_call(functools.partial(kernel, n_q, n_d, grp, scale_w, scale_r,...  37.5 us
    pallas_call x1, Pallas kernels, body(): pl.pallas_call(write_out, out_shape=shapes, in_specs=[vmem] * 3, out_spec...  0.82 us

profile of v2, /device:TPU:0, one launch (start us, length us, event | category | flops | bytes accessed | tf_op | source)
XLA Modules:
  0.0 39.0 jit_solution(14973359641640185886)
XLA Ops:
  0.6 37.5 %shard_map.148 = (f32[256,128]{1,0:T(8,128)S(1)}, f32[2,64,64]{2,1,0:T(8,128)S(1)}, f32[2,64,535]{2,1,0:T(8,128)S(1)}) custom-call(bf16[256,128]{1,0:T(8,128)(2,1)} %refs_0_.1, bf16[256,128]{1,0:T(8,128)(2,1)} %refs_1_.1, bf16[64,64]{1,0:T(8,128)(2,1)} %refs_2_.1, bf16[64,64]{1,0:T(8,128)(2,1)} %refs_3_.1, bf16[64,535]{1,0:T(8,128)(2,1)} %bitcast.5, ...), custom_call_target="tpu_custom_call" | custom-call | tf_op jit(solution)/shard_map/pallas_call | solution.py:510
  38.1 0.8 %shard_map.149 = (f32[256,128]{1,0:T(8,128)}, f32[2,64,64]{2,1,0:T(8,128)}, f32[2,64,535]{2,1,0:T(8,128)}) custom-call(f32[256,128]{1,0:T(8,128)S(1)} %get-tuple-element.9.refs_0_, f32[2,64,64]{2,1,0:T(8,128)S(1)} %get-tuple-element.10.refs_1_, f32[2,64,535]{2,1,0:T(8,128)S(1)} %get-tuple-element.11.refs_2_), custom_call_target="tpu_custom_call" | custom-call | tf_op jit(solution)/shard_map/pallas_call | solution.py:549

commit v3 on v2

--- a/solution.py
+++ b/solution.py
@@ -89,8 +89,9 @@
     x1,
     x2,
     req,
-    out1,
-    ghost1,
+    pub,
+    pubs,
+    pick_pub,
     out2,
     ghost2,
     ret_out2,
@@ -117,7 +118,8 @@
     feat = w1_ref.shape[0]
     rows, wide = h_ref.shape
     queries = wide // feat
-    send = ghost1.shape[0] // n_d
+    send = ghost2.shape[0] // n_d
+    slots = bnd_ref.shape[1]
     e_in = ein_ref.shape[1]
     e_bd = ebd_ref.shape[1]
     width = red_src.shape[3]
@@ -181,6 +183,23 @@
             own = pl.ds(pl.multiple_of(me_d * size, size), size)
             dst[own, :] = src[own, :]
 
+    def spread_start(phase, src, dst, size):
+        own = pl.ds(pl.multiple_of(me_d * size, size), size)
+
+        def go(i, carry):
+            pltpu.make_async_remote_copy(
+                src_ref=src,
+                dst_ref=dst.at[own],
+                send_sem=xsend.at[phase],
+                recv_sem=xrecv.at[phase],
+                device_id=(me_q, lax.rem(me_d + i, n_d)),
+                device_id_type=MESH,
+            ).start()
+            return carry
+
+        peer_loop(go)
+        dst[own, :] = src[...]
+
     def exchange_wait(phase, src, dst, size):
         some = pl.ds(0, (n_d - 1) * (size or 1))
         pltpu.make_async_remote_copy(
@@ -270,43 +289,44 @@
     spread = jnp.concatenate([gs_ref[...]] * per, axis=1)
     for p in range(n_d):
         gs_x[p] = spread[p : p + 1, :]
+    own_ids = lax.broadcasted_iota(jnp.int32, (rows, slots), 0)
+    row_of32 = jnp.where(own_ids == bnd_ref[...], 1.0, 0.0)
+    row_of = row_of32.astype(BF16)
+    pub[...] = dot_nn(row_of32.T.astype(BF16), h_ref[...]).astype(BF16)
 
     onehot_into(vt, ein_ref[1:2, :], 0, 64)
     onehot_into(vt, ebd_ref[1:2, :], e_in, 64)
     pl.semaphore_wait(barrier, greeted)
+    spread_start(1, pub, pubs, slots)
     exchange_start(0, gs_x, req, None)
+
+    lane_group = lax.broadcasted_iota(jnp.int32, (1, 128), 1) // send
+
+    def in_lanes(table):
+        parts = []
+        for j in range(n_d // per):
+            vec = jnp.zeros((1, 128), jnp.int32)
+            for k in range(per):
+                vec = jnp.where(lane_group == k, table[j * per + k, 0:1, :], vec)
+            parts.append(vec)
+        return jnp.concatenate(parts, axis=1)
+
+    ghost_peer = lax.broadcasted_iota(jnp.int32, (1, n_d * send), 1) // send
+    pick_rows = in_lanes(gs_x) + ghost_peer * slots
+    for j in range(n_d * send // 128):
+        ids = pick_rows[:, j * 128 : (j + 1) * 128]
+        for k in range(n_d * slots // 128):
+            row_ids = lax.broadcasted_iota(jnp.int32, (128, 128), 0) + k * 128
+            block = jnp.where(row_ids == ids, 1.0, 0.0).T
+            pick_pub[pl.ds(j * 128, 128), pl.ds(k * 128, 128)] = block.astype(BF16)
     onehot_into(st_in, ein_ref[0:1, :], 0, 64)
     onehot_into(st_bd, ebd_ref[0:1, :], 0, 64)
-
-    slots = bnd_ref.shape[1]
-    own_ids = lax.broadcasted_iota(jnp.int32, (rows, slots), 0)
-    row_of32 = jnp.where(own_ids == bnd_ref[...], 1.0, 0.0)
-    row_of = row_of32.astype(BF16)
-    published = dot_nn(row_of32.T.astype(BF16), h_ref[...]).astype(BF16)
-
-    exchange_wait(0, gs_x, req, None)
-    lane_group = lax.broadcasted_iota(jnp.int32, (1, 128), 1) // send
-    wanted = []
-    for j in range(n_d // per):
-        vec = jnp.zeros((1, 128), jnp.int32)
-        for k in range(per):
-            vec = jnp.where(lane_group == k, req[j * per + k, 0:1, :], vec)
-        wanted.append(vec)
-    wanted = jnp.concatenate(wanted, axis=1)
-    slot_ids = lax.broadcasted_iota(jnp.int32, (slots, n_d * send), 0)
-    slot_of32 = jnp.where(slot_ids == wanted, 1.0, 0.0)
-    slot_of_t = slot_of32.T.astype(BF16)
-    out1[...] = dot_nn(slot_of_t, published).astype(BF16)
-    exchange_start(1, out1, ghost1, send)
-
     onehot_into(rt, ein_ref[2:3, :], 0, 32)
     onehot_into(rt, ebd_ref[2:3, :], e_in, 32)
     relt[...] = jnp.zeros_like(relt)
     relt[pl.ds(0, feat), pl.ds(0, rel_count)] = r1_ref[...]
     relt[pl.ds(feat, feat), pl.ds(0, rel_count)] = r2_ref[...]
     rel_e[...] = dot_nn(relt[...], rt[...]).astype(BF16)
-    pick_t = dot_nn(row_of, slot_of32.astype(BF16)).astype(BF16)
-    pick = dot_nt(slot_of_t, row_of).astype(BF16)
 
     row_ids = lax.broadcasted_iota(jnp.int32, (feat, rows), 1) + me_d * rows
     lane_rel = lax.broadcasted_iota(jnp.int32, (feat, rel_count), 1)
@@ -348,9 +368,8 @@
             rstds.append(rstd)
         return summed_b, normed, rstds
 
-    def back_layer(up_t, normed, rstds, summed_b, w_ref):
-        wgrad = jnp.zeros((feat, feat), F32)
-        dsum = []
+    def back_layer(up_t, normed, rstds, w_ref):
+        dmixes, dsum = [], []
         for q in range(queries):
             y = normed[q]
             sig = jax.nn.sigmoid(y)
@@ -361,9 +380,15 @@
                 - y * jnp.mean(dact * y, axis=0, keepdims=True)
             )
             dmix_b = dmix.astype(BF16)
-            wgrad = wgrad + dot_nt(summed_b[q * feat : (q + 1) * feat], dmix_b)
+            dmixes.append(dmix_b)
             dsum.append(dot_nn(w_ref[...], dmix_b).astype(BF16))
-        return wgrad, jnp.concatenate(dsum, axis=0)
+        return dmixes, jnp.concatenate(dsum, axis=0)
+
+    def weight_grad(summed_b, dmixes):
+        wgrad = jnp.zeros((feat, feat), F32)
+        for q in range(queries):
+            wgrad = wgrad + dot_nt(summed_b[q * feat : (q + 1) * feat], dmixes[q])
+        return wgrad
 
     def rel_grad(downs, save):
         tots = []
@@ -380,16 +405,21 @@
         return both[:feat] + both[feat:]
 
     def table_grad(layer, down, onehot, lo, count):
-        message = split_hi_lo(down * rel_tile(layer, lo, count), 0)
-        both = dot_nt(onehot[...], message)
-        return both[:, :wide] + both[:, wide:]
+        message = (down * rel_tile(layer, lo, count)).astype(BF16)
+        return dot_nt(onehot[...], message)
 
     def give_back(ret_in):
         return dot_nn(pick_t, ret_in[...])
 
     sum1 = aggregate(0, h_t, st_in, x1, 0, e_in) + boost
-    exchange_wait(1, out1, ghost1, send)
-    sum1 = sum1 + aggregate(0, ghost1[...].astype(F32).T.astype(BF16), st_bd, x1, e_in, e_bd)
+    exchange_wait(0, gs_x, req, None)
+    slot_ids = lax.broadcasted_iota(jnp.int32, (slots, n_d * send), 0)
+    slot_of32 = jnp.where(slot_ids == in_lanes(req), 1.0, 0.0)
+    pick_t = dot_nn(row_of, slot_of32.astype(BF16)).astype(BF16)
+    pick = dot_nt(slot_of32.T.astype(BF16), row_of).astype(BF16)
+    exchange_wait(1, pubs, pubs, slots)
+    ghost1_t = dot_nn(pick_pub[...], pubs[...]).T.astype(BF16)
+    sum1 = sum1 + aggregate(0, ghost1_t, st_bd, x1, e_in, e_bd)
     sum1_b, norm1, rstd1 = normalise(sum1, w1_ref)
     h2_t = (
         jnp.concatenate([y * jax.nn.sigmoid(y) for y in norm1], axis=0) + h_t32
@@ -403,13 +433,13 @@
     sum2_b, norm2, rstd2 = normalise(sum2, w2_ref)
 
     cot32 = cot_ref[...].astype(F32)
-    wg2, dsum2 = back_layer(cot32.T, norm2, rstd2, sum2_b, w2_ref)
+    dmix2, dsum2 = back_layer(cot32.T, norm2, rstd2, w2_ref)
     down2_bd = dot_nn(dsum2, vt[:, pl.ds(e_in, e_bd)])
     ret_out2[...] = table_grad(1, down2_bd, st_bd, e_in, e_bd).astype(BF16)
     exchange_start(3, ret_out2, ret_in2, send)
     down2_in = dot_nn(dsum2, vt[:, pl.ds(0, e_in)])
     mid = cot32 + table_grad(1, down2_in, st_in, 0, e_in)
-    pack(1, rel_grad((down2_in, down2_bd), x2), wg2)
+    pack(1, rel_grad((down2_in, down2_bd), x2), weight_grad(sum2_b, dmix2))
     if RS_EARLY:
         scatter_start(1)
     exchange_wait(3, ret_out2, ret_in2, send)
@@ -417,10 +447,10 @@
         scatter_start(1)
     mid = mid + give_back(ret_in2)
 
-    wg1, dsum1 = back_layer(mid.T, norm1, rstd1, sum1_b, w1_ref)
+    dmix1, dsum1 = back_layer(mid.T, norm1, rstd1, w1_ref)
     down1_in = dot_nn(dsum1, vt[:, pl.ds(0, e_in)])
     down1_bd = dot_nn(dsum1, vt[:, pl.ds(e_in, e_bd)])
-    pack(0, rel_grad((down1_in, down1_bd), x1), wg1)
+    pack(0, rel_grad((down1_in, down1_bd), x1), weight_grad(sum1_b, dmix1))
     scatter_start(0)
     far_start(1)
     ret_out1[...] = table_grad(0, down1_bd, st_bd, e_in, e_bd).astype(BF16)
@@ -472,6 +502,7 @@
     n_q = lax.axis_size("query")
     send = ghost_slots.shape[1]
     ghosts = n_d * send
+    slots = bnd_rows.shape[0]
     e_in, e_bd = edges_in.shape[1], edges_bd.shape[1]
     edges = e_in + e_bd
     rel_pad = -(-(rel_count + 1) // 128) * 128
@@ -524,8 +555,9 @@
             pltpu.VMEM((wide, edges), BF16),
             pltpu.VMEM((wide, edges), BF16),
             pltpu.VMEM((n_d, 1, 128), jnp.int32),
-            pltpu.VMEM((ghosts, wide), BF16),
-            pltpu.VMEM((ghosts, wide), BF16),
+            pltpu.VMEM((slots, wide), BF16),
+            pltpu.VMEM((n_d * slots, wide), BF16),
+            pltpu.VMEM((ghosts, n_d * slots), BF16),
             pltpu.VMEM((ghosts, wide), BF16),
             pltpu.VMEM((ghosts, wide), BF16),
             pltpu.VMEM((ghosts, wide), BF16),

time: 39.2 us -> 39.9 us (1.018)
  Pallas kernels: 38.3 us -> 39 us
    pallas_call x1, Pallas kernels: 37.5 us -> 38.2 us  [body(): pl.pallas_call(functools.partial(kernel, n_q, n_d, grp, scale_w, scale_r,...]
where the time goes in v3:
time: 39.9 us; the launch traced here: 39.7 us
  Pallas kernels  39 us (98%)
  between operations  0.64 us (2%)
    pallas_call x1, Pallas kernels, body(): pl.pallas_call(functools.partial(kernel, n_q, n_d, grp, scale_w, scale_r,...  38.2 us
    pallas_call x1, Pallas kernels, body(): pl.pallas_call(write_out, out_shape=shapes, in_specs=[vmem] * 3, out_spec...  0.82 us

profile of v3, /device:TPU:0, one launch (start us, length us, event | category | flops | bytes accessed | tf_op | source)
XLA Modules:
  0.0 39.7 jit_solution(11810405796852860088)
XLA Ops:
  0.6 38.2 %shard_map.148 = (f32[256,128]{1,0:T(8,128)S(1)}, f32[2,64,64]{2,1,0:T(8,128)S(1)}, f32[2,64,535]{2,1,0:T(8,128)S(1)}) custom-call(bf16[256,128]{1,0:T(8,128)(2,1)} %refs_0_.1, bf16[256,128]{1,0:T(8,128)(2,1)} %refs_1_.1, bf16[64,64]{1,0:T(8,128)(2,1)} %refs_2_.1, bf16[64,64]{1,0:T(8,128)(2,1)} %refs_3_.1, bf16[64,535]{1,0:T(8,128)(2,1)} %bitcast.5, ...), custom_call_target="tpu_custom_call" | custom-call | tf_op jit(solution)/shard_map/pallas_call | solution.py:541
  38.9 0.8 %shard_map.149 = (f32[256,128]{1,0:T(8,128)}, f32[2,64,64]{2,1,0:T(8,128)}, f32[2,64,535]{2,1,0:T(8,128)}) custom-call(f32[256,128]{1,0:T(8,128)S(1)} %get-tuple-element.9.refs_0_, f32[2,64,64]{2,1,0:T(8,128)S(1)} %get-tuple-element.10.refs_1_, f32[2,64,535]{2,1,0:T(8,128)S(1)} %get-tuple-element.11.refs_2_), custom_call_target="tpu_custom_call" | custom-call | tf_op jit(solution)/shard_map/pallas_call | solution.py:581

commit v4 on v2

--- a/solution.py
+++ b/solution.py
@@ -11,7 +11,6 @@
 MESH = pl.DeviceIdType.MESH
 F32 = jnp.float32
 BF16 = jnp.bfloat16
-RS_EARLY = False
 
 
 def dot_nn(a, b):
@@ -122,6 +121,14 @@
     e_bd = ebd_ref.shape[1]
     width = red_src.shape[3]
 
+    def peer_loop(step):
+        if n_d <= 32:
+            order = sorted(range(1, n_d), key=lambda i: -min(i // grp, n_far - i // grp))
+            for i in order:
+                step(i, 0)
+        else:
+            lax.fori_loop(1, n_d, step, 0)
+
     barrier = pltpu.get_barrier_semaphore()
 
     def greet(i, carry):
@@ -129,7 +136,7 @@
         pl.semaphore_signal(barrier, inc=1, device_id=(me_q, t), device_id_type=MESH)
         return carry
 
-    loop(1, n_d, greet)
+    peer_loop(greet)
     for dq in range(1, n_q):
         for k in range(grp):
             pl.semaphore_signal(
@@ -148,14 +155,6 @@
     for load in loads[::-1]:
         load.wait()
 
-    def peer_loop(step):
-        if n_d <= 32:
-            order = sorted(range(1, n_d), key=lambda i: -min(i // grp, n_far - i // grp))
-            for i in order:
-                step(i, 0)
-        else:
-            lax.fori_loop(1, n_d, step, 0)
-
     def exchange_start(phase, src, dst, size):
         def go(i, carry):
             peer = lax.rem(me_d + i, n_d)
@@ -348,9 +347,8 @@
             rstds.append(rstd)
         return summed_b, normed, rstds
 
-    def back_layer(up_t, normed, rstds, summed_b, w_ref):
-        wgrad = jnp.zeros((feat, feat), F32)
-        dsum = []
+    def back_layer(up_t, normed, rstds, w_ref):
+        dmixes, dsum = [], []
         for q in range(queries):
             y = normed[q]
             sig = jax.nn.sigmoid(y)
@@ -361,9 +359,15 @@
                 - y * jnp.mean(dact * y, axis=0, keepdims=True)
             )
             dmix_b = dmix.astype(BF16)
-            wgrad = wgrad + dot_nt(summed_b[q * feat : (q + 1) * feat], dmix_b)
+            dmixes.append(dmix_b)
             dsum.append(dot_nn(w_ref[...], dmix_b).astype(BF16))
-        return wgrad, jnp.concatenate(dsum, axis=0)
+        return dmixes, jnp.concatenate(dsum, axis=0)
+
+    def weight_grad(summed_b, dmixes):
+        wgrad = jnp.zeros((feat, feat), F32)
+        for q in range(queries):
+            wgrad = wgrad + dot_nt(summed_b[q * feat : (q + 1) * feat], dmixes[q])
+        return wgrad
 
     def rel_grad(downs, save):
         tots = []
@@ -380,9 +384,8 @@
         return both[:feat] + both[feat:]
 
     def table_grad(layer, down, onehot, lo, count):
-        message = split_hi_lo(down * rel_tile(layer, lo, count), 0)
-        both = dot_nt(onehot[...], message)
-        return both[:, :wide] + both[:, wide:]
+        message = (down * rel_tile(layer, lo, count)).astype(BF16)
+        return dot_nt(onehot[...], message)
 
     def give_back(ret_in):
         return dot_nn(pick_t, ret_in[...])
@@ -403,24 +406,21 @@
     sum2_b, norm2, rstd2 = normalise(sum2, w2_ref)
 
     cot32 = cot_ref[...].astype(F32)
-    wg2, dsum2 = back_layer(cot32.T, norm2, rstd2, sum2_b, w2_ref)
+    dmix2, dsum2 = back_layer(cot32.T, norm2, rstd2, w2_ref)
     down2_bd = dot_nn(dsum2, vt[:, pl.ds(e_in, e_bd)])
     ret_out2[...] = table_grad(1, down2_bd, st_bd, e_in, e_bd).astype(BF16)
     exchange_start(3, ret_out2, ret_in2, send)
     down2_in = dot_nn(dsum2, vt[:, pl.ds(0, e_in)])
+    pack(1, rel_grad((down2_in, down2_bd), x2), weight_grad(sum2_b, dmix2))
+    scatter_start(1)
     mid = cot32 + table_grad(1, down2_in, st_in, 0, e_in)
-    pack(1, rel_grad((down2_in, down2_bd), x2), wg2)
-    if RS_EARLY:
-        scatter_start(1)
     exchange_wait(3, ret_out2, ret_in2, send)
-    if not RS_EARLY:
-        scatter_start(1)
     mid = mid + give_back(ret_in2)
 
-    wg1, dsum1 = back_layer(mid.T, norm1, rstd1, sum1_b, w1_ref)
+    dmix1, dsum1 = back_layer(mid.T, norm1, rstd1, w1_ref)
     down1_in = dot_nn(dsum1, vt[:, pl.ds(0, e_in)])
     down1_bd = dot_nn(dsum1, vt[:, pl.ds(e_in, e_bd)])
-    pack(0, rel_grad((down1_in, down1_bd), x1), wg1)
+    pack(0, rel_grad((down1_in, down1_bd), x1), weight_grad(sum1_b, dmix1))
     scatter_start(0)
     far_start(1)
     ret_out1[...] = table_grad(0, down1_bd, st_bd, e_in, e_bd).astype(BF16)

time: 39.2 us -> 38.8 us (0.990)
  Pallas kernels: 38.3 us -> 37.9 us
    pallas_call x1, Pallas kernels: 37.5 us -> 37.1 us  [body(): pl.pallas_call(functools.partial(kernel, n_q, n_d, grp, scale_w, scale_r,...]
where the time goes in v4:
time: 38.8 us; the launch traced here: 38.5 us
  Pallas kernels  37.9 us (98%)
  between operations  0.64 us (2%)
    pallas_call x1, Pallas kernels, body(): pl.pallas_call(functools.partial(kernel, n_q, n_d, grp, scale_w, scale_r,...  37.1 us
    pallas_call x1, Pallas kernels, body(): pl.pallas_call(write_out, out_shape=shapes, in_specs=[vmem] * 3, out_spec...  0.82 us

profile of v4, /device:TPU:0, one launch (start us, length us, event | category | flops | bytes accessed | tf_op | source)
XLA Modules:
  0.0 38.5 jit_solution(14866006723236663631)
XLA Ops:
  0.6 37.1 %shard_map.148 = (f32[256,128]{1,0:T(8,128)S(1)}, f32[2,64,64]{2,1,0:T(8,128)S(1)}, f32[2,64,535]{2,1,0:T(8,128)S(1)}) custom-call(bf16[256,128]{1,0:T(8,128)(2,1)} %refs_0_.1, bf16[256,128]{1,0:T(8,128)(2,1)} %refs_1_.1, bf16[64,64]{1,0:T(8,128)(2,1)} %refs_2_.1, bf16[64,64]{1,0:T(8,128)(2,1)} %refs_3_.1, bf16[64,535]{1,0:T(8,128)(2,1)} %bitcast.5, ...), custom_call_target="tpu_custom_call" | custom-call | tf_op jit(solution)/shard_map/pallas_call | solution.py:510
  37.7 0.8 %shard_map.149 = (f32[256,128]{1,0:T(8,128)}, f32[2,64,64]{2,1,0:T(8,128)}, f32[2,64,535]{2,1,0:T(8,128)}) custom-call(f32[256,128]{1,0:T(8,128)S(1)} %get-tuple-element.9.refs_0_, f32[2,64,64]{2,1,0:T(8,128)S(1)} %get-tuple-element.10.refs_1_, f32[2,64,535]{2,1,0:T(8,128)S(1)} %get-tuple-element.11.refs_2_), custom_call_target="tpu_custom_call" | custom-call | tf_op jit(solution)/shard_map/pallas_call | solution.py:549

commit v5 on v4

--- a/solution.py
+++ b/solution.py
@@ -378,10 +378,9 @@
             tot = prod[:feat]
             for q in range(1, queries):
                 tot = tot + prod[q * feat : (q + 1) * feat]
-            tots.append(split_hi_lo(tot, 0))
+            tots.append(tot.astype(BF16))
             lo += count
-        both = dot_nt(jnp.concatenate(tots, axis=1), rt[pl.ds(0, rel_rows), :])
-        return both[:feat] + both[feat:]
+        return dot_nt(jnp.concatenate(tots, axis=1), rt[pl.ds(0, rel_rows), :])
 
     def table_grad(layer, down, onehot, lo, count):
         message = (down * rel_tile(layer, lo, count)).astype(BF16)

time: 38.8 us -> 38.6 us (level)
  no operation moved by 1% of the time
where the time goes in v5:
time: 38.6 us; the launch traced here: 38.3 us
  Pallas kernels  37.7 us (98%)
  between operations  0.64 us (2%)
    pallas_call x1, Pallas kernels, body(): pl.pallas_call(functools.partial(kernel, n_q, n_d, grp, scale_w, scale_r,...  36.8 us
    pallas_call x1, Pallas kernels, body(): pl.pallas_call(write_out, out_shape=shapes, in_specs=[vmem] * 3, out_spec...  0.82 us

profile of v5, /device:TPU:0, one launch (start us, length us, event | category | flops | bytes accessed | tf_op | source)
XLA Modules:
  0.0 38.3 jit_solution(11421935310074357353)
XLA Ops:
  0.6 36.8 %shard_map.148 = (f32[256,128]{1,0:T(8,128)S(1)}, f32[2,64,64]{2,1,0:T(8,128)S(1)}, f32[2,64,535]{2,1,0:T(8,128)S(1)}) custom-call(bf16[256,128]{1,0:T(8,128)(2,1)} %refs_0_.1, bf16[256,128]{1,0:T(8,128)(2,1)} %refs_1_.1, bf16[64,64]{1,0:T(8,128)(2,1)} %refs_2_.1, bf16[64,64]{1,0:T(8,128)(2,1)} %refs_3_.1, bf16[64,535]{1,0:T(8,128)(2,1)} %bitcast.5, ...), custom_call_target="tpu_custom_call" | custom-call | tf_op jit(solution)/shard_map/pallas_call | solution.py:509
  37.5 0.8 %shard_map.149 = (f32[256,128]{1,0:T(8,128)}, f32[2,64,64]{2,1,0:T(8,128)}, f32[2,64,535]{2,1,0:T(8,128)}) custom-call(f32[256,128]{1,0:T(8,128)S(1)} %get-tuple-element.9.refs_0_, f32[2,64,64]{2,1,0:T(8,128)S(1)} %get-tuple-element.10.refs_1_, f32[2,64,535]{2,1,0:T(8,128)S(1)} %get-tuple-element.11.refs_2_), custom_call_target="tpu_custom_call" | custom-call | tf_op jit(solution)/shard_map/pallas_call | solution.py:548

commit v6 on v5

--- a/solution.py
+++ b/solution.py
@@ -96,6 +96,8 @@
     ret_in2,
     ret_out1,
     ret_in1,
+    cot_t,
+    slope1,
     red_src,
     red_in,
     red_z,
@@ -347,12 +349,15 @@
             rstds.append(rstd)
         return summed_b, normed, rstds
 
-    def back_layer(up_t, normed, rstds, w_ref):
+    def silu_slope(y):
+        sig = jax.nn.sigmoid(y)
+        return sig * (1.0 + y * (1.0 - sig))
+
+    def back_layer(up_t, slopes, normed, rstds, w_ref):
         dmixes, dsum = [], []
         for q in range(queries):
             y = normed[q]
-            sig = jax.nn.sigmoid(y)
-            dact = up_t[q * feat : (q + 1) * feat] * sig * (1.0 + y * (1.0 - sig))
+            dact = up_t[q * feat : (q + 1) * feat] * slopes[q]
             dmix = rstds[q] * (
                 dact
                 - jnp.mean(dact, axis=0, keepdims=True)
@@ -383,7 +388,8 @@
         return dot_nt(jnp.concatenate(tots, axis=1), rt[pl.ds(0, rel_rows), :])
 
     def table_grad(layer, down, onehot, lo, count):
-        message = (down * rel_tile(layer, lo, count)).astype(BF16)
+        part = rel_e[pl.ds(layer * feat, feat), pl.ds(lo, count)]
+        message = down.astype(BF16) * jnp.concatenate([part] * queries, axis=0)
         return dot_nt(onehot[...], message)
 
     def give_back(ret_in):
@@ -400,12 +406,15 @@
     out2[...] = dot_nt(pick, h2_t).astype(BF16)
     exchange_start(2, out2, ghost2, send)
     sum2 = aggregate(1, h2_t, st_in, x2, 0, e_in) + boost
+    cot32 = cot_ref[...].astype(F32)
+    cot_t[...] = cot32.T
+    for q in range(queries):
+        slope1[pl.ds(q * feat, feat), :] = silu_slope(norm1[q])
     exchange_wait(2, out2, ghost2, send)
     sum2 = sum2 + aggregate(1, ghost2[...].astype(F32).T.astype(BF16), st_bd, x2, e_in, e_bd)
     sum2_b, norm2, rstd2 = normalise(sum2, w2_ref)
 
-    cot32 = cot_ref[...].astype(F32)
-    dmix2, dsum2 = back_layer(cot32.T, norm2, rstd2, w2_ref)
+    dmix2, dsum2 = back_layer(cot_t[...], [silu_slope(y) for y in norm2], norm2, rstd2, w2_ref)
     down2_bd = dot_nn(dsum2, vt[:, pl.ds(e_in, e_bd)])
     ret_out2[...] = table_grad(1, down2_bd, st_bd, e_in, e_bd).astype(BF16)
     exchange_start(3, ret_out2, ret_in2, send)
@@ -416,7 +425,8 @@
     exchange_wait(3, ret_out2, ret_in2, send)
     mid = mid + give_back(ret_in2)
 
-    dmix1, dsum1 = back_layer(mid.T, norm1, rstd1, w1_ref)
+    slopes1 = [slope1[pl.ds(q * feat, feat), :] for q in range(queries)]
+    dmix1, dsum1 = back_layer(mid.T, slopes1, norm1, rstd1, w1_ref)
     down1_in = dot_nn(dsum1, vt[:, pl.ds(0, e_in)])
     down1_bd = dot_nn(dsum1, vt[:, pl.ds(e_in, e_bd)])
     pack(0, rel_grad((down1_in, down1_bd), x1), weight_grad(sum1_b, dmix1))
@@ -531,6 +541,8 @@
             pltpu.VMEM((ghosts, wide), BF16),
             pltpu.VMEM((ghosts, wide), BF16),
             pltpu.VMEM((ghosts, wide), BF16),
+            pltpu.VMEM((wide, rows), F32),
+            pltpu.VMEM((wide, rows), F32),
             pltpu.VMEM((2, n_near, part, width), BF16),
             pltpu.VMEM((2, n_near, part, width), BF16),
             pltpu.VMEM((2, n_far, part, width), BF16),

time: 38.6 us -> 38.6 us (level)
  no operation moved by 1% of the time
where the time goes in v6:
time: 38.6 us; the launch traced here: 38.3 us
  Pallas kernels  37.7 us (98%)
  between operations  0.64 us (2%)
    pallas_call x1, Pallas kernels, body(): pl.pallas_call(functools.partial(kernel, n_q, n_d, grp, scale_w, scale_r,...  36.8 us
    pallas_call x1, Pallas kernels, body(): pl.pallas_call(write_out, out_shape=shapes, in_specs=[vmem] * 3, out_spec...  0.82 us

profile of v6, /device:TPU:0, one launch (start us, length us, event | category | flops | bytes accessed | tf_op | source)
XLA Modules:
  0.0 38.3 jit_solution(3749748400152787302)
XLA Ops:
  0.6 36.8 %shard_map.148 = (f32[256,128]{1,0:T(8,128)S(1)}, f32[2,64,64]{2,1,0:T(8,128)S(1)}, f32[2,64,535]{2,1,0:T(8,128)S(1)}) custom-call(bf16[256,128]{1,0:T(8,128)(2,1)} %refs_0_.1, bf16[256,128]{1,0:T(8,128)(2,1)} %refs_1_.1, bf16[64,64]{1,0:T(8,128)(2,1)} %refs_2_.1, bf16[64,64]{1,0:T(8,128)(2,1)} %refs_3_.1, bf16[64,535]{1,0:T(8,128)(2,1)} %bitcast.5, ...), custom_call_target="tpu_custom_call" | custom-call | tf_op jit(solution)/shard_map/pallas_call | solution.py:519
  37.5 0.8 %shard_map.149 = (f32[256,128]{1,0:T(8,128)}, f32[2,64,64]{2,1,0:T(8,128)}, f32[2,64,535]{2,1,0:T(8,128)}) custom-call(f32[256,128]{1,0:T(8,128)S(1)} %get-tuple-element.9.refs_0_, f32[2,64,64]{2,1,0:T(8,128)S(1)} %get-tuple-element.10.refs_1_, f32[2,64,535]{2,1,0:T(8,128)S(1)} %get-tuple-element.11.refs_2_), custom_call_target="tpu_custom_call" | custom-call | tf_op jit(solution)/shard_map/pallas_call | solution.py:560

commit v7 on v6

--- a/solution.py
+++ b/solution.py
@@ -383,9 +383,10 @@
             tot = prod[:feat]
             for q in range(1, queries):
                 tot = tot + prod[q * feat : (q + 1) * feat]
-            tots.append(tot.astype(BF16))
+            tots.append(split_hi_lo(tot, 0))
             lo += count
-        return dot_nt(jnp.concatenate(tots, axis=1), rt[pl.ds(0, rel_rows), :])
+        both = dot_nt(jnp.concatenate(tots, axis=1), rt[pl.ds(0, rel_rows), :])
+        return both[:feat] + both[feat:]
 
     def table_grad(layer, down, onehot, lo, count):
         part = rel_e[pl.ds(layer * feat, feat), pl.ds(lo, count)]

time: 38.6 us -> 38.8 us (level)
  no operation moved by 1% of the time
where the time goes in v7:
time: 38.8 us; the launch traced here: 38.5 us
  Pallas kernels  37.9 us (98%)
  between operations  0.64 us (2%)
    pallas_call x1, Pallas kernels, body(): pl.pallas_call(functools.partial(kernel, n_q, n_d, grp, scale_w, scale_r,...  37.1 us
    pallas_call x1, Pallas kernels, body(): pl.pallas_call(write_out, out_shape=shapes, in_specs=[vmem] * 3, out_spec...  0.82 us

profile of v7, /device:TPU:0, one launch (start us, length us, event | category | flops | bytes accessed | tf_op | source)
XLA Modules:
  0.0 38.5 jit_solution(7964112832021314240)
XLA Ops:
  0.6 37.1 %shard_map.148 = (f32[256,128]{1,0:T(8,128)S(1)}, f32[2,64,64]{2,1,0:T(8,128)S(1)}, f32[2,64,535]{2,1,0:T(8,128)S(1)}) custom-call(bf16[256,128]{1,0:T(8,128)(2,1)} %refs_0_.1, bf16[256,128]{1,0:T(8,128)(2,1)} %refs_1_.1, bf16[64,64]{1,0:T(8,128)(2,1)} %refs_2_.1, bf16[64,64]{1,0:T(8,128)(2,1)} %refs_3_.1, bf16[64,535]{1,0:T(8,128)(2,1)} %bitcast.5, ...), custom_call_target="tpu_custom_call" | custom-call | tf_op jit(solution)/shard_map/pallas_call | solution.py:520
  37.7 0.8 %shard_map.149 = (f32[256,128]{1,0:T(8,128)}, f32[2,64,64]{2,1,0:T(8,128)}, f32[2,64,535]{2,1,0:T(8,128)}) custom-call(f32[256,128]{1,0:T(8,128)S(1)} %get-tuple-element.9.refs_0_, f32[2,64,64]{2,1,0:T(8,128)S(1)} %get-tuple-element.10.refs_1_, f32[2,64,535]{2,1,0:T(8,128)S(1)} %get-tuple-element.11.refs_2_), custom_call_target="tpu_custom_call" | custom-call | tf_op jit(solution)/shard_map/pallas_call | solution.py:561

commit v8 on v5

--- a/solution.py
+++ b/solution.py
@@ -152,7 +152,7 @@
     ]
     for load in loads[::-1]:
         load.start()
-    for load in loads[::-1]:
+    for load in loads[10:]:
         load.wait()
 
     def exchange_start(phase, src, dst, size):
@@ -274,6 +274,8 @@
     onehot_into(vt, ebd_ref[1:2, :], e_in, 64)
     pl.semaphore_wait(barrier, greeted)
     exchange_start(0, gs_x, req, None)
+    for load in loads[:10]:
+        load.wait()
     onehot_into(st_in, ein_ref[0:1, :], 0, 64)
     onehot_into(st_bd, ebd_ref[0:1, :], 0, 64)
 

time: 38.6 us -> 38.5 us (level)
  no operation moved by 1% of the time
where the time goes in v8:
time: 38.5 us; the launch traced here: 38.3 us
  Pallas kernels  37.7 us (98%)
  between operations  0.64 us (2%)
    pallas_call x1, Pallas kernels, body(): pl.pallas_call(functools.partial(kernel, n_q, n_d, grp, scale_w, scale_r,...  36.8 us
    pallas_call x1, Pallas kernels, body(): pl.pallas_call(write_out, out_shape=shapes, in_specs=[vmem] * 3, out_spec...  0.82 us

profile of v8, /device:TPU:0, one launch (start us, length us, event | category | flops | bytes accessed | tf_op | source)
XLA Modules:
  0.0 38.3 jit_solution(10670608428132717458)
XLA Ops:
  0.6 36.8 %shard_map.148 = (f32[256,128]{1,0:T(8,128)S(1)}, f32[2,64,64]{2,1,0:T(8,128)S(1)}, f32[2,64,535]{2,1,0:T(8,128)S(1)}) custom-call(bf16[256,128]{1,0:T(8,128)(2,1)} %refs_0_.1, bf16[256,128]{1,0:T(8,128)(2,1)} %refs_1_.1, bf16[64,64]{1,0:T(8,128)(2,1)} %refs_2_.1, bf16[64,64]{1,0:T(8,128)(2,1)} %refs_3_.1, bf16[64,535]{1,0:T(8,128)(2,1)} %bitcast.5, ...), custom_call_target="tpu_custom_call" | custom-call | tf_op jit(solution)/shard_map/pallas_call | solution.py:511
  37.5 0.8 %shard_map.149 = (f32[256,128]{1,0:T(8,128)}, f32[2,64,64]{2,1,0:T(8,128)}, f32[2,64,535]{2,1,0:T(8,128)}) custom-call(f32[256,128]{1,0:T(8,128)S(1)} %get-tuple-element.9.refs_0_, f32[2,64,64]{2,1,0:T(8,128)S(1)} %get-tuple-element.10.refs_1_, f32[2,64,535]{2,1,0:T(8,128)S(1)} %get-tuple-element.11.refs_2_), custom_call_target="tpu_custom_call" | custom-call | tf_op jit(solution)/shard_map/pallas_call | solution.py:550
